TPU v7x, 32 devices: a whole 2x2x4 slice. The times are simulated.
32 devices in a mesh: inst: 2 (over core), pipe: 4 (over z), tensor: 4 (over y, x).
Axes of the slice: x: 2, y: 2, z: 4, core: 2. Of those that a mesh axis runs over, the one named last changes fastest.
Arguments:
- lengths: int32 [2, 64], replicated, may hold values from 2 to 384, as said below
- page_table: int32 [2, 64, 3], P('inst'), may hold values from 0 to 191, as said below
- migration: int32 [16, 3], replicated, may hold values from 0 to 63, as said below
- dest_slots: int32 [16, 3], replicated, may hold values from 0 to 47, as said below
- queries: bfloat16 [2, 4, 64, 8192], P('inst', 'pipe', None, 'tensor'), may hold values from -64 to 64
- key_cache: bfloat16 [2, 4, 8, 24576, 128], P('inst', 'pipe', 'tensor'), may hold values from -64 to 64
- value_cache: bfloat16 [2, 4, 8, 24576, 128], P('inst', 'pipe', 'tensor'), may hold values from -5 to 5
- out_weight: bfloat16 [4, 8192, 8192], P('pipe', 'tensor'), may hold values from -0.09375 to 0.09375
Outputs:
- update: bfloat16 [2, 64, 8192], P('inst', None, ('pipe', 'tensor'))
- received_keys: bfloat16 [2, 4, 8, 6144, 128], P('inst', 'pipe', 'tensor')
- received_values: bfloat16 [2, 4, 8, 6144, 128], P('inst', 'pipe', 'tensor')
Inputs may be any that keep to these rules, and one draw needn't show every extreme that they name: `lengths`: in instance 1 every request holds more than 192 tokens and one holds exactly 384; in instance 0 every request holds at most 192. `page_table`: for each instance a permutation of its 192 pool pages, 3 for each request. `migration`: rows 0 to 7 name source instance 1 and destination instance 0, the other rows source 0 and destination 1; the requests of all rows are distinct numbers, and the one in row 0 holds at most (2) * 128 tokens. `dest_slots`: A permutation of the 48 receive slots.
All inputs are finite; a program needn't handle non-finite values.
Results may differ from a plain program's by a relative error of at most 0.018.
Values may be sent and summed in bfloat16 or wider, within the bound.
A program may use at most 128 MiB of HBM per device.

v0:
```python
import math

import jax
import jax.numpy as jnp
from jax import lax
from jax.sharding import PartitionSpec as P

PAGE = 128


def from_partner(array, axis, stride):
    return lax.ppermute(array, axis, [(i, i ^ 1 << stride) for i in range(lax.axis_size(axis))])


def attend(query_block, key_pages, value_pages, page_map, length_list, page_bound):
    row_count, kv_heads, group_size, head_dim = query_block.shape
    page_size = key_pages.shape[2]
    scale_factor = 1.0 / math.sqrt(head_dim)
    offsets = jnp.arange(page_size, dtype=jnp.int32)

    def advance(page_index, carry):
        running_max, running_sum, accumulated = carry
        slot_ids = lax.dynamic_index_in_dim(page_map, page_index, 1, keepdims=False)
        key_block = key_pages[:, slot_ids]
        value_block = value_pages[:, slot_ids]
        scores = (
            jnp.einsum(
                "rkgd,krtd->rkgt", query_block, key_block, preferred_element_type=jnp.float32
            )
            * scale_factor
        )
        visible = ((page_index * page_size + offsets)[None, :] < length_list[:, None])[
            :, None, None, :
        ]
        scores = jnp.where(visible, scores, -1e30)
        new_max = jnp.maximum(running_max, jnp.max(scores, axis=-1))
        fading = jnp.exp(running_max - new_max)
        weights = jnp.where(visible, jnp.exp(scores - new_max[..., None]), 0.0)
        running_sum = running_sum * fading + jnp.sum(weights, axis=-1)
        accumulated = accumulated * fading[..., None] + jnp.einsum(
            "rkgt,krtd->rkgd",
            weights,
            value_block.astype(jnp.float32),
            precision=lax.Precision.HIGHEST,
        )
        return (new_max, running_sum, accumulated)

    initial = (
        jnp.full((row_count, kv_heads, group_size), -1e30, jnp.float32),
        jnp.zeros((row_count, kv_heads, group_size), jnp.float32),
        jnp.zeros((row_count, kv_heads, group_size, head_dim), jnp.float32),
    )
    running_max, running_sum, accumulated = lax.fori_loop(0, page_bound, advance, initial)
    return (
        (accumulated / running_sum[..., None])
        .reshape(row_count, kv_heads * group_size * head_dim)
        .astype(jnp.bfloat16)
    )


def body(lengths, page_table, migration, dest_slots, queries, key_cache, value_cache, out_weight):
    kv_heads = key_cache.shape[2]
    head_dim = key_cache.shape[4]
    row_count = page_table.shape[1]
    max_pages = page_table.shape[2]
    pool_pages = key_cache.shape[3] // PAGE
    group_size = queries.shape[3] // head_dim // kv_heads
    myself = lax.axis_index("inst")
    movers = migration[:, 0]
    sources = migration[:, 1]
    outgoing_rows = sources == myself
    own_lengths = lax.dynamic_index_in_dim(lengths, myself, 0, keepdims=False)
    moved_lengths = lengths[sources, movers]
    page_map = page_table[0]
    key_pages = key_cache[0, 0].reshape(kv_heads, pool_pages, PAGE, head_dim)
    value_pages = value_cache[0, 0].reshape(kv_heads, pool_pages, PAGE, head_dim)
    live_pages = (
        (jnp.arange(max_pages, dtype=jnp.int32)[None, :] * PAGE < moved_lengths[:, None])
        & outgoing_rows[:, None]
    ).reshape(-1)
    out_slots = page_map[movers].reshape(-1)
    outgoing_keys = jnp.where(
        live_pages[None, :, None, None], key_pages[:, out_slots], jnp.zeros((), key_cache.dtype)
    )
    outgoing_values = jnp.where(
        live_pages[None, :, None, None], value_pages[:, out_slots], jnp.zeros((), value_cache.dtype)
    )
    query_block = queries[0, 0].reshape(row_count, kv_heads, group_size, head_dim)
    got_keys, got_values = from_partner((outgoing_keys, outgoing_values), "inst", 0)
    local_bound = (jnp.max(own_lengths) + PAGE - 1) // PAGE
    attended = attend(query_block, key_pages, value_pages, page_map, own_lengths, local_bound)
    recv_slots = dest_slots.reshape(-1)
    recv_count = recv_slots.shape[0]
    received_keys = (
        jnp.zeros((kv_heads, recv_count, PAGE, head_dim), key_cache.dtype)
        .at[:, recv_slots]
        .set(got_keys)
    )
    received_values = (
        jnp.zeros((kv_heads, recv_count, PAGE, head_dim), value_cache.dtype)
        .at[:, recv_slots]
        .set(got_values)
    )
    layer_term = jnp.dot(attended, out_weight[0], preferred_element_type=jnp.float32)
    partial_total = lax.psum_scatter(
        layer_term.astype(jnp.bfloat16), "pipe", scatter_dimension=1, tiled=True
    )
    summed = lax.psum_scatter(partial_total, "tensor", scatter_dimension=1, tiled=True).astype(
        jnp.float32
    )
    update = summed.astype(jnp.bfloat16)[None]
    received_keys = received_keys.reshape(1, 1, kv_heads, recv_count * PAGE, head_dim)
    received_values = received_values.reshape(1, 1, kv_heads, recv_count * PAGE, head_dim)
    return (update, received_keys, received_values)


def solution(mesh):
    placed = (
        P(),
        P("inst", None, None),
        P(),
        P(),
        P("inst", "pipe", None, "tensor"),
        P("inst", "pipe", "tensor", None, None),
        P("inst", "pipe", "tensor", None, None),
        P("pipe", "tensor", None),
    )
    return jax.shard_map(
        body,
        mesh=mesh,
        in_specs=placed,
        out_specs=(
            P("inst", None, ("pipe", "tensor")),
            P("inst", "pipe", "tensor", None, None),
            P("inst", "pipe", "tensor", None, None),
        ),
        check_vma=False,
    )
```

profile of v0, /device:TPU:0, one launch (start us, length us, event | category | flops | bytes accessed | tf_op | source)
XLA Modules:
  0.0 186.2 jit_solution(16008434692302925080)
XLA Ops:
  7.2 0.0 reduce-scatter.3.cloned.1.call-start
  7.2 0.8 copy.14
  8.0 0.8 fusion.36
  8.8 0.6 gather_fusion.3
  9.3 0.1 reshape.134
  9.4 5.7 %gather_fusion.4 = bf16[48,2,128,128]{3,2,1,0:T(8,128)(2,1)S(1)} fusion(bf16[2,192,128,128]{3,2,1,0:T(8,128)(2,1)} %bitcast.86, s32[1024]{0:T(1024)S(1)} %pad_clamp_fusion.1), kind=kCustom, calls=%fused_computation.4 | custom fusion | bytes 6291648 | tf_op jit(solution)/shard_map/gather | solution.py:83
  15.2 0.0 copy-start
  15.2 7.3 %gather_fusion.5 = bf16[48,2,128,128]{3,2,1,0:T(8,128)(2,1)} fusion(bf16[2,192,128,128]{3,2,1,0:T(8,128)(2,1)} %bitcast.88, s32[1024]{0:T(1024)S(1)} %pad_clamp_fusion.1), kind=kCustom, calls=%fused_computation.5 | custom fusion | bytes 6291648 | tf_op jit(solution)/shard_map/gather | solution.py:86
  22.5 0.7 compare_bitcast_fusion
  23.2 0.7 gather_fusion.2
  23.9 0.1 compare_and_fusion
  23.9 0.1 and.27
  24.1 0.0 copy-start.3
  24.1 5.3 %select_bitcast_fusion = (bf16[2,48,128,128]{3,2,0,1:T(8,128)(2,1)}, bf16[2,48,128,128]{3,2,0,1:T(8,128)(2,1)}) fusion(bf16[48,2,128,128]{3,2,1,0:T(8,128)(2,1)} %gather_fusion.5, pred[48]{0:T(512)(128)(4,1)S(1)} %and.27, bf16[48,2,128,128]{3,2,1,0:T(8,128)(2,1)S(1)} %gather_fusion.4), kind=kLoop, calls=%fused_computation.33 | loop fusion | flops 3145728 | bytes 12582960 | tf_op jit(solution)/shard_map/jit(_where)/select_n | solution.py:85
  29.4 0.5 collective-permute-start
  29.9 0.0 collective-permute-start.1
  29.9 0.6 fusion.37
  31.2 0.1 copy.15
  31.4 51.3 %while.15 = (s32[]{:T(128)}, f32[64,2,8]{2,1,0:T(2,128)S(1)}, f32[64,2,8]{2,1,0:T(2,128)S(1)}, f32[64,2,8,128]{3,2,1,0:T(8,128)S(1)}, s32[]{:T(128)}, /*index=5*...) while((s32[]{:T(128)}, f32[64,2,8]{2,1,0:T(2,128)S(1)}, ...), condition=%wide.region_4.5_spmd.clone, body=%wide.region_1.4_spmd.clone.sunk | while | flops 236203328 | bytes 28154556 | solution.py:53
  31.5 7.6 %gather_fusion = bf16[64,2,128,128]{3,2,1,0:T(8,128)(2,1)} fusion(bf16[2,192,128,128]{3,2,1,0:T(8,128)(2,1)} %get-tuple-element.246, s32[1024]{0:T(1024)S(1)} %pad_clamp_fusion.4), kind=kCustom, calls=%fused_computation.clone.clone.1 | custom fusion | bytes 8388864 | tf_op jit(solution)/shard_map/while/body/gather | solution.py:24
  39.1 0.1 broadcast_compare_fusion.2
  39.1 4.6 %fusion.51 = (f32[64,2,8]{2,1,0:T(2,128)S(1)}, f32[64,2,8,128]{3,2,1,0:T(8,128)S(1)}) fusion(bf16[64,2,8,128]{3,2,1,0:T(8,128)(2,1)S(1)} %get-tuple-element.247, bf16[64,2,128,128]{3,2,1,0:T(8,128)(2,1)} %gather_fusion, pred[64,128]{1,0:T(8,128)(4,1)S(1)} %broadcast_compare_fusion.2), kind=kOutput, calls=%fused_computation.57.clone.1 | convolution fusion | flops 33946624 | bytes 4993024 | tf_op jit(solution)/shard_map/while/body/rkgd,krtd->rkgt/dot_general | solution.py:27
  43.8 0.4 fusion.52
  44.2 7.6 %gather_fusion.1 = bf16[64,2,128,128]{3,2,1,0:T(8,128)(2,1)} fusion(bf16[2,192,128,128]{3,2,1,0:T(8,128)(2,1)} %get-tuple-element.248, s32[1024]{0:T(1024)S(1)} %pad_clamp_fusion.4), kind=kCustom, calls=%fused_computation.1.clone.clone.1 | custom fusion | bytes 8388864 | tf_op jit(solution)/shard_map/while/body/gather | solution.py:25
  51.8 5.2 %fusion.53 = f32[64,2,8,128]{3,2,1,0:T(8,128)S(1)} fusion(bf16[64,2,128,128]{3,2,1,0:T(8,128)(2,1)} %gather_fusion.1, f32[64,2,8,128]{3,2,1,0:T(8,128)S(1)} %get-tuple-element.228, f32[64,2,8,128]{3,2,1,0:T(8,128)S(1)} %get-tuple-element.208, f32[64,2,8]{2,1,0:T(2,128)S(1)} %bitcast.98, f32[64,2,8]{2,1,0:T(2,128)S(1)} %max.5, ...), kind=kOutput, calls=%fused_computation.13.clone.1 | convolution fusion | flops 201850880 | bytes 5783552 | tf_op jit(solution)/shard_map/while/body/rkgt,krtd->rkgd/dot_general | solution.py:40
  57.1 7.6 %gather_fusion = bf16[64,2,128,128]{3,2,1,0:T(8,128)(2,1)} fusion(bf16[2,192,128,128]{3,2,1,0:T(8,128)(2,1)} %get-tuple-element.246, s32[1024]{0:T(1024)S(1)} %pad_clamp_fusion.4), kind=kCustom, calls=%fused_computation.clone.clone.1 | custom fusion | bytes 8388864 | tf_op jit(solution)/shard_map/while/body/gather | solution.py:24
  64.7 0.1 broadcast_compare_fusion.2
  64.8 4.6 %fusion.51 = (f32[64,2,8]{2,1,0:T(2,128)S(1)}, f32[64,2,8,128]{3,2,1,0:T(8,128)S(1)}) fusion(bf16[64,2,8,128]{3,2,1,0:T(8,128)(2,1)S(1)} %get-tuple-element.247, bf16[64,2,128,128]{3,2,1,0:T(8,128)(2,1)} %gather_fusion, pred[64,128]{1,0:T(8,128)(4,1)S(1)} %broadcast_compare_fusion.2), kind=kOutput, calls=%fused_computation.57.clone.1 | convolution fusion | flops 33946624 | bytes 4993024 | tf_op jit(solution)/shard_map/while/body/rkgd,krtd->rkgt/dot_general | solution.py:27
  69.4 0.4 fusion.52
  69.9 7.6 %gather_fusion.1 = bf16[64,2,128,128]{3,2,1,0:T(8,128)(2,1)} fusion(bf16[2,192,128,128]{3,2,1,0:T(8,128)(2,1)} %get-tuple-element.248, s32[1024]{0:T(1024)S(1)} %pad_clamp_fusion.4), kind=kCustom, calls=%fused_computation.1.clone.clone.1 | custom fusion | bytes 8388864 | tf_op jit(solution)/shard_map/while/body/gather | solution.py:25
  77.5 5.2 %fusion.53 = f32[64,2,8,128]{3,2,1,0:T(8,128)S(1)} fusion(bf16[64,2,128,128]{3,2,1,0:T(8,128)(2,1)} %gather_fusion.1, f32[64,2,8,128]{3,2,1,0:T(8,128)S(1)} %get-tuple-element.228, f32[64,2,8,128]{3,2,1,0:T(8,128)S(1)} %get-tuple-element.208, f32[64,2,8]{2,1,0:T(2,128)S(1)} %bitcast.98, f32[64,2,8]{2,1,0:T(2,128)S(1)} %max.5, ...), kind=kOutput, calls=%fused_computation.13.clone.1 | convolution fusion | flops 201850880 | bytes 5783552 | tf_op jit(solution)/shard_map/while/body/rkgt,krtd->rkgd/dot_general | solution.py:40
  82.7 0.2 divide_convert_fusion
  82.9 0.0 copy-start.4
  83.0 14.7 %fusion.26 = bf16[64,8192]{1,0:T(8,128)(2,1)} fusion(bf16[1,2048,8192]{2,1,0:T(8,128)(2,1)} %param.17, bf16[8,8,16,128]{3,2,1,0:T(8,128)(2,1)S(1)} %bitcast.99), kind=kOutput, calls=%fused_computation.32 | convolution fusion | flops 2148007936 | bytes 34865152 | tf_op jit(solution)/shard_map/dot_general | solution.py:104
  97.6 0.0 reduce-scatter.3.cloned.1.call-update
  97.7 0.2 reduce-scatter.5.cloned.1.call-start
  97.9 55.2 %reduce-scatter.3.cloned.1.call-done = bf16[64,2048]{1,0:T(8,128)(2,1)} async-done(((bf16[64,8192]{1,0:T(8,128)(2,1)}), bf16[64,2048]{1,0:T(8,128)(2,1)}) %reduce-scatter.3.cloned.1.call-update) | async-done | bytes 262160 | tf_op jit(solution)/shard_map/reduce_scatter | solution.py:105
  153.1 0.0 reduce-scatter.5.cloned.1.call-update
  153.2 0.1 copy.16
  153.3 0.1 reshape.133
  153.4 0.8 broadcast.108.clone
  154.1 6.6 %scatter_fusion = bf16[2,48,128,128]{3,2,1,0:T(8,128)(2,1)S(1)} fusion(bf16[2,48,128,128]{3,2,1,0:T(8,128)(2,1)S(1)} %broadcast.108.clone, s32[48]{0:T(128)S(1)} %fusion.31, bf16[48,2,128,128]{3,2,1,0:T(8,128)(2,1)} %bitcast.12), kind=kCustom, calls=%fused_computation.6 | custom fusion | bytes 9437376 | tf_op jit(solution)/shard_map/scatter | solution.py:97
  160.8 0.0 copy-start.2
  160.8 1.6 copy-done.2
  162.4 0.8 broadcast.108.clone.1
  163.2 6.6 %scatter_fusion.1 = bf16[2,48,128,128]{3,2,1,0:T(8,128)(2,1)S(1)} fusion(bf16[2,48,128,128]{3,2,1,0:T(8,128)(2,1)S(1)} %broadcast.108.clone.1, s32[48]{0:T(128)S(1)} %fusion.31, bf16[48,2,128,128]{3,2,1,0:T(8,128)(2,1)} %bitcast.15), kind=kCustom, calls=%fused_computation.7 | custom fusion | bytes 9437376 | tf_op jit(solution)/shard_map/scatter | solution.py:102
  169.9 0.0 copy-start.1
  169.9 9.5 %reduce-scatter.5.cloned.1.call-done = bf16[64,512]{1,0:T(8,128)(2,1)} async-done(((bf16[64,2048]{1,0:T(8,128)(2,1)}), bf16[64,512]{1,0:T(8,128)(2,1)}) %reduce-scatter.5.cloned.1.call-update) | async-done | bytes 65552 | tf_op jit(solution)/shard_map/reduce_scatter | solution.py:108
  (27 shorter events, 0.4 us)
Async XLA Ops:
  7.2 146.0 %reduce-scatter.3.cloned.1.call-start = ((), (), s32[]{:S(2)}) async-start(), calls=%async_computation.2 | async-start | bytes 1310720 | tf_op jit(solution)/shard_map/reduce_scatter | solution.py:105
  15.2 8.0 %copy-start = (s32[2,64]{1,0:T(2,128)S(1)}, s32[2,64]{1,0:T(2,128)}, u32[]{:S(2)}) copy-start(s32[2,64]{1,0:T(2,128)} %param.10) | copy-start | bytes 1540
  24.1 7.2 %copy-start.3 = (bf16[1,1,64,2048]{3,2,1,0:T(8,128)(2,1)S(1)}, bf16[1,1,64,2048]{3,2,1,0:T(8,128)(2,1)}, u32[]{:S(2)}) copy-start(bf16[1,1,64,2048]{3,2,1,0:T(8,128)(2,1)} %param.14) | copy-start | bytes 786436
  29.4 124.0 %collective-permute-start = (bf16[2,48,128,128]{3,2,0,1:T(8,128)(2,1)}, bf16[2,48,128,128]{3,2,0,1:T(8,128)(2,1)}, u32[]{:S(2)}, u32[]{:S(2)}) collective-permute-start(bf16[2,48,128,128]{3,2,0,1:T(8,128)(2,1)} %get-tuple-element.136), channel_id=1, source_target_pairs={{0,16},{16,0},{1,17},{17,1},{2,18},{18,2},{3,19},{19,3},{4,20},{20... | collective-permute-start | bytes 9437192 | tf_op jit(solution)/shard_map/ppermute | solution.py:12
  29.9 130.9 %collective-permute-start.1 = (bf16[2,48,128,128]{3,2,0,1:T(8,128)(2,1)}, bf16[2,48,128,128]{3,2,0,1:T(8,128)(2,1)}, u32[]{:S(2)}, u32[]{:S(2)}) collective-permute-start(bf16[2,48,128,128]{3,2,0,1:T(8,128)(2,1)} %get-tuple-element.135), channel_id=1, source_target_pairs={{0,16},{16,0},{1,17},{17,1},{2,18},{18,2},{3,19},{19,3},{4,20},{20... | collective-permute-start | bytes 9437192 | tf_op jit(solution)/shard_map/ppermute | solution.py:12
  82.9 70.2 %copy-start.4 = (s32[16,3]{0,1:T(4,128)S(1)}, s32[16,3]{0,1:T(4,128)}, u32[]{:S(2)}) copy-start(s32[16,3]{0,1:T(4,128)} %param.13) | copy-start | bytes 580
  97.7 81.7 %reduce-scatter.5.cloned.1.call-start = ((), (), s32[]{:S(2)}) async-start(), calls=%async_computation.3 | async-start | bytes 327680 | tf_op jit(solution)/shard_map/reduce_scatter | solution.py:108
  160.8 1.7 copy-start.2
  169.9 9.5 %copy-start.1 = (bf16[2,48,128,128]{3,2,1,0:T(8,128)(2,1)}, bf16[2,48,128,128]{3,2,1,0:T(8,128)(2,1)S(1)}, u32[]{:S(2)}) copy-start(bf16[2,48,128,128]{3,2,1,0:T(8,128)(2,1)S(1)} %scatter_fusion.1) | copy-start | bytes 9437188
Sparse Core Ops, SparseCore 0:
  97.8 55.3 reduce-scatter.2
  156.5 22.8 reduce-scatter.4
where the time goes:
time: 187 us; the launch traced here: 186 us
  waiting for transfers between devices  64.7 us (35%)
  local copies, waits for them, and re-layouts  62.5 us (33%)
  matrix products  34.2 us (18%)
  between operations  14.9 us (8%)
  other arithmetic  8.88 us (5%)
    reduce_scatter x1, waiting for transfers between devices, body(): lax.psum_scatter(layer_term.astype(jnp.bfloat16), 'pipe', scatter_dimensi...  55.2 us
    gather x2, local copies, waits for them, and re-layouts, advance(): key_block = key_pages[:, slot_ids]  15.2 us
    gather x2, local copies, waits for them, and re-layouts, advance(): value_block = value_pages[:, slot_ids]  15.2 us
    dot_general x1, matrix products, body(): jnp.dot(attended, out_weight[0], preferred_element_type=jnp.float32)  14.7 us
    dot_general x2, matrix products, advance(): jnp.einsum('rkgt,krtd->rkgd', weights, value_block.astype(jnp.float32), p...  10.4 us
    reduce_scatter x1, waiting for transfers between devices, body(): lax.psum_scatter(partial_total, 'tensor', scatter_dimension=1, tiled=True)  9.46 us
    dot_general x2, matrix products, advance(): jnp.einsum('rkgd,krtd->rkgt', query_block, key_block, preferred_element_t...  9.16 us
    gather x1, local copies, waits for them, and re-layouts, body(): value_pages[:, out_slots]  7.3 us
  transfers between devices with their start and end apart: 4, of which 2 were waited for; matrix products, arithmetic and copies ran while one was open for 44% of the time, Pallas kernels for 0%

commit v1 on v0

v1 whole, which is shorter than its diff:
```python
import functools
import math

import jax
import jax.numpy as jnp
from jax import lax
from jax.experimental import pallas as pl
from jax.experimental.pallas import tpu as pltpu
from jax.sharding import PartitionSpec as P

PAGE = 128
SLOTS = 16
UNROLL = 2
MESH = pl.DeviceIdType.MESH


def from_partner(array, axis, stride):
    return lax.ppermute(array, axis, [(i, i ^ 1 << stride) for i in range(lax.axis_size(axis))])


def attend_kernel(
    length_ref, table_ref, migration_ref, dest_ref, query_ref, key_ref, value_ref,
    out_ref, key_area, value_area,
    key_buf, value_buf, move_buf, zero_buf, page_sem, move_sem,
):
    rows, max_pages = table_ref.shape
    moves = migration_ref.shape[0]
    kv_heads, _, page, head_dim = key_ref.shape
    heads = query_ref.shape[1]
    group = heads // kv_heads
    tokens = max_pages * page
    scale = 1.0 / math.sqrt(head_dim)
    me = lax.axis_index("inst")

    def page_copies(row, index):
        slot = lax.rem(row, SLOTS)
        source = table_ref[row, index]
        place = pl.ds(index * page, page)
        return (
            pltpu.make_async_copy(
                key_ref.at[:, source], key_buf.at[slot, :, place], page_sem.at[slot, index, 0]
            ),
            pltpu.make_async_copy(
                value_ref.at[:, source], value_buf.at[slot, :, place], page_sem.at[slot, index, 1]
            ),
        )

    def each_page(row, act):
        for index in range(max_pages):
            @pl.when(index * page < length_ref[me, row])
            def _():
                for copy in page_copies(row, index):
                    act(copy)

    def each_move(act):
        @pl.loop(0, moves)
        def _(move):
            row, source = migration_ref[move, 0], migration_ref[move, 1]
            for index in range(max_pages):
                live = (source == me) & (index * page < length_ref[source, row])
                slot = dest_ref[move, index]
                act(move, index, live, table_ref[row, index], slot)

    def load_move(move, index, pool_page):
        return [
            pltpu.make_async_copy(
                ref.at[:, pool_page], move_buf.at[move, index, which], move_sem.at[move, index, which]
            )
            for which, ref in enumerate((key_ref, value_ref))
        ]

    def store_move(move, index, slot):
        return [
            pltpu.make_async_copy(
                move_buf.at[move, index, which], area.at[:, slot], move_sem.at[move, index, which]
            )
            for which, area in enumerate((key_area, value_area))
        ]

    def clear_move(move, index, slot):
        return [
            pltpu.make_async_copy(zero_buf, area.at[:, slot], move_sem.at[move, index, which])
            for which, area in enumerate((key_area, value_area))
        ]

    zero_buf[...] = jnp.zeros_like(zero_buf)

    @pl.loop(0, SLOTS)
    def _(slot):
        value_buf[slot] = jnp.zeros(value_buf.shape[1:], value_buf.dtype)

    @pl.loop(0, SLOTS)
    def _(row):
        each_page(row, lambda copy: copy.start())

    def begin_move(move, index, live, pool_page, slot):
        @pl.when(live)
        def _():
            for copy in load_move(move, index, pool_page):
                copy.start()

        @pl.when(jnp.logical_not(live))
        def _():
            for copy in clear_move(move, index, slot):
                copy.start()

    each_move(begin_move)

    position = lax.broadcasted_iota(jnp.int32, (heads, tokens), 1)

    def attend_row(row):
        slot = lax.rem(row, SLOTS)
        keys = key_buf[slot].reshape(kv_heads * tokens, head_dim)
        values = value_buf[slot].reshape(kv_heads * tokens, head_dim)
        full = lax.dot_general(
            query_ref[row], keys, (((1,), (1,)), ((), ())), preferred_element_type=jnp.float32
        )
        scores = jnp.concatenate(
            [
                full[k * group : (k + 1) * group, k * tokens : (k + 1) * tokens]
                for k in range(kv_heads)
            ],
            axis=0,
        )
        scores = jnp.where(position < length_ref[me, row], scores * scale, -1e30)
        weights = jnp.exp(scores - jnp.max(scores, axis=-1, keepdims=True))
        total = jnp.sum(weights, axis=-1, keepdims=True)
        nothing = jnp.zeros((group, tokens), jnp.float32)
        spread = jnp.concatenate(
            [
                jnp.concatenate(
                    [
                        weights[k * group : (k + 1) * group] if at == k else nothing
                        for at in range(kv_heads)
                    ],
                    axis=1,
                )
                for k in range(kv_heads)
            ],
            axis=0,
        )
        mixed = jnp.dot(
            spread.astype(jnp.bfloat16), values, preferred_element_type=jnp.float32
        )
        return (mixed / total).astype(out_ref.dtype)

    steps = rows // UNROLL

    @pl.loop(0, steps)
    def _(step):
        for u in range(UNROLL):
            each_page(step * UNROLL + u, lambda copy: copy.wait())
        results = [attend_row(step * UNROLL + u) for u in range(UNROLL)]
        for u in range(UNROLL):
            out_ref[step * UNROLL + u] = results[u]
        for u in range(UNROLL):
            @pl.when(step * UNROLL + u + SLOTS < rows)
            def _():
                each_page(step * UNROLL + u + SLOTS, lambda copy: copy.start())

        @pl.when(step == steps // 2)
        def _():
            def turn_move(move, index, live, pool_page, slot):
                @pl.when(live)
                def _():
                    for copy in load_move(move, index, pool_page):
                        copy.wait()
                    for copy in store_move(move, index, slot):
                        copy.start()

            each_move(turn_move)

    def end_move(move, index, live, pool_page, slot):
        for copy in clear_move(move, index, slot):
            copy.wait()

    each_move(end_move)


def attend(lengths, page_table, migration, dest_slots, queries, key_pages, value_pages):
    rows, max_pages = page_table.shape
    moves = migration.shape[0]
    kv_heads, _, page, head_dim = key_pages.shape
    heads = queries.shape[1]
    area = jax.ShapeDtypeStruct((kv_heads, moves * max_pages, page, head_dim), key_pages.dtype)
    smem = pl.BlockSpec(memory_space=pltpu.SMEM)
    vmem = pl.BlockSpec(memory_space=pltpu.VMEM)
    hbm = pl.BlockSpec(memory_space=pl.ANY)
    return pl.pallas_call(
        attend_kernel,
        out_shape=(jax.ShapeDtypeStruct(queries.shape, queries.dtype), area, area),
        in_specs=[smem] * 4 + [vmem, hbm, hbm],
        out_specs=(vmem, hbm, hbm),
        scratch_shapes=[
            pltpu.VMEM((SLOTS, kv_heads, max_pages * page, head_dim), key_pages.dtype),
            pltpu.VMEM((SLOTS, kv_heads, max_pages * page, head_dim), key_pages.dtype),
            pltpu.VMEM((moves, max_pages, 2, kv_heads, page, head_dim), key_pages.dtype),
            pltpu.VMEM((kv_heads, page, head_dim), key_pages.dtype),
            pltpu.SemaphoreType.DMA((SLOTS, max_pages, 2)),
            pltpu.SemaphoreType.DMA((moves, max_pages, 2)),
        ],
        name="attend",
    )(lengths, page_table, migration, dest_slots, queries, key_pages, value_pages)


def project_kernel(
    pipes, tensors, attended_ref, weight_ref, out_ref,
    weight_buf, send_one, recv_one, own, send_two, recv_two,
    weight_sem, send_one_sem, recv_one_sem, send_two_sem, recv_two_sem,
):
    my_pipe = lax.axis_index("pipe")
    my_tensor = lax.axis_index("tensor")
    blocks = pipes * tensors
    width = out_ref.shape[1]

    def target(block):
        chunk, turn = block // tensors, lax.rem(block, tensors)
        to_pipe = lax.rem(my_pipe + pipes - 1 - chunk, pipes)
        to_tensor = lax.rem(my_tensor + 1 + turn, tensors)
        return chunk, turn, to_pipe, to_tensor

    def weight_copy(block):
        _, _, to_pipe, to_tensor = target(block)
        start = pl.multiple_of((to_pipe * tensors + to_tensor) * width, width)
        return pltpu.make_async_copy(
            weight_ref.at[:, pl.ds(start, width)], weight_buf.at[block], weight_sem.at[block]
        )

    def first_copy(chunk, turn, to_tensor):
        return pltpu.make_async_remote_copy(
            src_ref=send_one.at[chunk, turn],
            dst_ref=recv_one.at[chunk, turn],
            send_sem=send_one_sem.at[chunk, turn],
            recv_sem=recv_one_sem.at[chunk, turn],
            device_id={"tensor": to_tensor},
            device_id_type=MESH,
        )

    def second_copy(chunk, to_pipe):
        return pltpu.make_async_remote_copy(
            src_ref=send_two.at[chunk],
            dst_ref=recv_two.at[chunk],
            send_sem=send_two_sem.at[chunk],
            recv_sem=recv_two_sem.at[chunk],
            device_id={"pipe": to_pipe},
            device_id_type=MESH,
        )

    @pl.loop(0, blocks)
    def _(block):
        weight_copy(block).start()

    barrier = pltpu.get_barrier_semaphore()
    for step in range(1, tensors):
        pl.semaphore_signal(
            barrier, inc=1, device_id={"tensor": lax.rem(my_tensor + step, tensors)},
            device_id_type=MESH,
        )
    for step in range(1, pipes):
        pl.semaphore_signal(
            barrier, inc=1, device_id={"pipe": lax.rem(my_pipe + step, pipes)},
            device_id_type=MESH,
        )
    pl.semaphore_wait(barrier, tensors + pipes - 2)

    def gathered(chunk):
        total = own[chunk]
        for turn in range(tensors - 1):
            first_copy(chunk, turn, my_tensor).wait_recv()
            total = total + recv_one[chunk, turn].astype(jnp.float32)
        return total

    @pl.loop(0, blocks)
    def _(block):
        chunk, turn, _, to_tensor = target(block)
        weight_copy(block).wait()
        term = jnp.dot(
            attended_ref[...], weight_buf[block], preferred_element_type=jnp.float32
        )

        @pl.when(turn < tensors - 1)
        def _():
            send_one[chunk, turn] = term.astype(send_one.dtype)
            first_copy(chunk, turn, to_tensor).start()

        @pl.when(turn == tensors - 1)
        def _():
            own[chunk] = term

        @pl.when((turn == tensors - 1) & (chunk > 0))
        def _():
            before = chunk - 1
            send_two[before] = gathered(before).astype(send_two.dtype)
            second_copy(before, lax.rem(my_pipe + pipes - 1 - before, pipes)).start()

    total = gathered(pipes - 1)
    for chunk in range(pipes - 1):
        second_copy(chunk, my_pipe).wait_recv()
        total = total + recv_two[chunk].astype(jnp.float32)
    out_ref[...] = total.astype(out_ref.dtype)

    for chunk in range(pipes):
        for turn in range(tensors - 1):
            first_copy(chunk, turn, my_tensor).wait_send()
    for chunk in range(pipes - 1):
        second_copy(chunk, my_pipe).wait_send()


def project(attended, weight):
    pipes, tensors = lax.axis_size("pipe"), lax.axis_size("tensor")
    rows, depth = attended.shape
    columns = weight.shape[1]
    width = columns // (pipes * tensors)
    return pl.pallas_call(
        functools.partial(project_kernel, pipes, tensors),
        out_shape=jax.ShapeDtypeStruct((rows, width), jnp.bfloat16),
        in_specs=[pl.BlockSpec(memory_space=pltpu.VMEM), pl.BlockSpec(memory_space=pl.ANY)],
        out_specs=pl.BlockSpec(memory_space=pltpu.VMEM),
        scratch_shapes=[
            pltpu.VMEM((pipes * tensors, depth, width), weight.dtype),
            pltpu.VMEM((pipes, tensors - 1, rows, width), jnp.bfloat16),
            pltpu.VMEM((pipes, tensors - 1, rows, width), jnp.bfloat16),
            pltpu.VMEM((pipes, rows, width), jnp.float32),
            pltpu.VMEM((pipes - 1, rows, width), jnp.bfloat16),
            pltpu.VMEM((pipes - 1, rows, width), jnp.bfloat16),
            pltpu.SemaphoreType.DMA((pipes * tensors,)),
            pltpu.SemaphoreType.DMA((pipes, tensors - 1)),
            pltpu.SemaphoreType.DMA((pipes, tensors - 1)),
            pltpu.SemaphoreType.DMA((pipes - 1,)),
            pltpu.SemaphoreType.DMA((pipes - 1,)),
        ],
        cost_estimate=pl.CostEstimate(
            flops=2 * rows * depth * columns,
            bytes_accessed=2 * depth * columns,
            transcendentals=0,
        ),
        compiler_params=pltpu.CompilerParams(
            collective_id=0, has_side_effects=True, vmem_limit_bytes=48 * 1024 * 1024
        ),
        name="project",
    )(attended, weight)


def body(lengths, page_table, migration, dest_slots, queries, key_cache, value_cache, out_weight):
    kv_heads = key_cache.shape[2]
    head_dim = key_cache.shape[4]
    row_count = page_table.shape[1]
    pool_pages = key_cache.shape[3] // PAGE
    heads = queries.shape[3] // head_dim
    key_pages = key_cache[0, 0].reshape(kv_heads, pool_pages, PAGE, head_dim)
    value_pages = value_cache[0, 0].reshape(kv_heads, pool_pages, PAGE, head_dim)
    query_block = queries[0, 0].reshape(row_count, heads, head_dim)
    attended, key_area, value_area = attend(
        lengths, page_table[0], migration, dest_slots, query_block, key_pages, value_pages
    )
    got_keys, got_values = from_partner((key_area, value_area), "inst", 0)
    update = project(attended.reshape(row_count, heads * head_dim), out_weight[0])
    shape = (1, 1, kv_heads, got_keys.shape[1] * PAGE, head_dim)
    return (update[None], got_keys.reshape(shape), got_values.reshape(shape))


def solution(mesh):
    placed = (
        P(),
        P("inst", None, None),
        P(),
        P(),
        P("inst", "pipe", None, "tensor"),
        P("inst", "pipe", "tensor", None, None),
        P("inst", "pipe", "tensor", None, None),
        P("pipe", "tensor", None),
    )
    return jax.shard_map(
        body,
        mesh=mesh,
        in_specs=placed,
        out_specs=(
            P("inst", None, ("pipe", "tensor")),
            P("inst", "pipe", "tensor", None, None),
            P("inst", "pipe", "tensor", None, None),
        ),
        check_vma=False,
    )
```

time: 187 us -> 62 us (0.33)
  waiting for transfers between devices: 64.7 us -> 0.01 us
  local copies, waits for them, and re-layouts: 62.5 us -> 10.7 us
  Pallas kernels: 0 us -> 49.2 us
  matrix products: 34.2 us -> 0 us
  between operations: 14.9 us -> 0.67 us
  other arithmetic: 8.88 us -> 0 us
    reduce_scatter x2 -> x0, waiting for transfers between devices: 64.7 us -> none  [the longest x1 55.2 us: body(): lax.psum_scatter(layer_term.astype(jnp.bfloat16), 'pipe', scatter_dimensi...]
    pallas_call x0 -> x2, Pallas kernels: none -> 49.2 us  [the longest x1 27.5 us: attend(): pl.pallas_call(attend_kernel, out_shape=(jax.ShapeDtypeStruct(queries.sha...]
    gather x8 -> x0, local copies, waits for them, and re-layouts: 44.7 us -> none  [the longest x2 15.2 us: advance(): key_block = key_pages[:, slot_ids]]
    dot_general x5 -> x0, matrix products: 34.2 us -> none  [the longest x1 14.7 us: body(): jnp.dot(attended, out_weight[0], preferred_element_type=jnp.float32)]
    scatter x2 -> x0, local copies, waits for them, and re-layouts: 13.3 us -> none  [the longest x1 6.64 us: body(): received_values = jnp.zeros((kv_heads, recv_count, PAGE, head_dim), value...]
    unnamed x14 -> x8, local copies, waits for them, and re-layouts: 2.65 us -> 10.7 us
    select_n x5 -> x0, other arithmetic: 5.32 us -> none  [the longest x1 5.29 us: body(): jnp.where(live_pages[None, :, None, None], value_pages[:, out_slots], jnp...]
  transfers between devices with their start and end apart: 4 -> 2, of which waited for: 2 -> 0; matrix products, arithmetic and copies ran while one was open for 44% -> 2% of each run, Pallas kernels for 0% -> 35%
where the time goes in v1:
time: 62 us; the launch traced here: 61.6 us
  Pallas kernels  49.2 us (79%)
  local copies, waits for them, and re-layouts  10.7 us (17%)
  starting transfers between devices  0.99 us (2%)
  between operations  0.67 us (1%)
    pallas_call x1, Pallas kernels, attend(): pl.pallas_call(attend_kernel, out_shape=(jax.ShapeDtypeStruct(queries.sha...  27.5 us
    pallas_call x1, Pallas kernels, project(): pl.pallas_call(functools.partial(project_kernel, pipes, tensors), out_sha...  21.7 us
    unnamed x8, local copies, waits for them, and re-layouts  10.7 us
  transfers between devices with their start and end apart: 2, of which 0 were waited for; matrix products, arithmetic and copies ran while one was open for 2% of the time, Pallas kernels for 35%

profile of v1, /device:TPU:0, one launch (start us, length us, event | category | flops | bytes accessed | tf_op | source)
XLA Modules:
  0.0 61.6 jit_solution(3561263901762034025)
XLA Ops:
  0.6 1.4 %copy.12.migration_ref = s32[16,3]{1,0:T(8,128)} copy(s32[16,3]{0,1:T(4,128)} %param.10) | data formatting | bytes 384 | tf_op args[2]
  2.0 1.4 %copy.13.dest_ref = s32[16,3]{1,0:T(8,128)} copy(s32[16,3]{0,1:T(4,128)} %param.11) | data formatting | bytes 384 | tf_op args[3]
  3.3 1.4 %copy.11 = s32[1,64,3]{2,1,0:T(8,128)} copy(s32[1,64,3]{1,0,2:T(1,128)} %param.9) | data formatting | bytes 1536 | tf_op args[1]
  4.7 1.7 %copy.14 = bf16[8,8,16,128]{3,2,1,0:T(8,128)(2,1)} copy(bf16[8,8,16,128]{3,1,2,0:T(8,128)(2,1)} %bitcast.23) | data formatting | bytes 524288
  6.4 27.5 %attend.1 = (bf16[64,16,128]{2,1,0:T(8,128)(2,1)}, bf16[2,48,128,128]{3,2,1,0:T(8,128)(2,1)}, bf16[2,48,128,128]{3,2,1,0:T(8,128)(2,1)}) custom-call(s32[2,64]{1,0:T(2,128)} %length_ref.1, s32[64,3]{1,0:T(8,128)} %bitcast.25, s32[16,3]{1,0:T(8,128)} %copy.12.migration_ref, s32[16,3]{1,0:T(8,128)} %copy.13.dest_ref, bf16[64,16,128]{2,1,0:T(8,128)(2,1)} %bitcast.22, ...), custom_call_target="tpu_custom_call" | custom-call | tf_op jit(solution)/shard_map/attend/pallas_call | solution.py:189
  33.9 0.9 %collective-permute-start = (bf16[2,48,128,128]{3,2,1,0:T(8,128)(2,1)}, bf16[2,48,128,128]{3,2,1,0:T(8,128)(2,1)S(1)}, u32[]{:S(2)}, u32[]{:S(2)}) collective-permute-start(bf16[2,48,128,128]{3,2,1,0:T(8,128)(2,1)} %get-tuple-element.7), channel_id=1, source_target_pairs={{0,16},{16,0},{1,17},{17,1},{2,18},{18,2},{3,19},{19,3},{4,20},{20... | collective-permute-start | bytes 9437192 | tf_op jit(solution)/shard_map/ppermute | solution.py:18
  34.9 0.1 collective-permute-start.1
  34.9 1.0 %copy.17 = bf16[8,8,16,128]{3,1,2,0:T(8,128)(2,1)S(1)} copy(bf16[8,8,16,128]{3,2,1,0:T(8,128)(2,1)} %bitcast.24) | data formatting | bytes 524288
  36.0 21.7 %project.1 = bf16[64,512]{1,0:T(8,128)(2,1)S(1)} custom-call(bf16[64,2048]{1,0:T(8,128)(2,1)S(1)} %bitcast.15, bf16[2048,8192]{1,0:T(8,128)(2,1)} %bitcast.17), custom_call_target="tpu_custom_call" | custom-call | flops 2147483648 | bytes 33554432 | tf_op jit(solution)/shard_map/project/pallas_call | solution.py:314
  57.7 0.0 collective-permute-done
  57.7 0.0 collective-permute-done.1
  57.7 0.6 %copy.21 = bf16[1,64,512]{2,1,0:T(8,128)(2,1)} copy(bf16[1,64,512]{2,1,0:T(8,128)(2,1)S(1)} %bitcast.16) | data formatting | bytes 131072
  58.3 1.7 %copy.22 = bf16[1,1,2,6144,128]{4,3,2,1,0:T(8,128)(2,1)} copy(bf16[1,1,2,6144,128]{4,3,2,1,0:T(8,128)(2,1)S(1)} %bitcast.20) | data formatting | bytes 6291456
  60.0 1.7 %copy.23 = bf16[1,1,2,6144,128]{4,3,2,1,0:T(8,128)(2,1)} copy(bf16[1,1,2,6144,128]{4,3,2,1,0:T(8,128)(2,1)S(1)} %bitcast.21) | data formatting | bytes 6291456
Async XLA Ops:
  33.9 23.7 %collective-permute-start = (bf16[2,48,128,128]{3,2,1,0:T(8,128)(2,1)}, bf16[2,48,128,128]{3,2,1,0:T(8,128)(2,1)S(1)}, u32[]{:S(2)}, u32[]{:S(2)}) collective-permute-start(bf16[2,48,128,128]{3,2,1,0:T(8,128)(2,1)} %get-tuple-element.7), channel_id=1, source_target_pairs={{0,16},{16,0},{1,17},{17,1},{2,18},{18,2},{3,19},{19,3},{4,20},{20... | collective-permute-start | bytes 9437192 | tf_op jit(solution)/shard_map/ppermute | solution.py:18
  34.9 22.8 %collective-permute-start.1 = (bf16[2,48,128,128]{3,2,1,0:T(8,128)(2,1)}, bf16[2,48,128,128]{3,2,1,0:T(8,128)(2,1)S(1)}, u32[]{:S(2)}, u32[]{:S(2)}) collective-permute-start(bf16[2,48,128,128]{3,2,1,0:T(8,128)(2,1)} %get-tuple-element.8), channel_id=1, source_target_pairs={{0,16},{16,0},{1,17},{17,1},{2,18},{18,2},{3,19},{19,3},{4,20},{20... | collective-permute-start | bytes 9437192 | tf_op jit(solution)/shard_map/ppermute | solution.py:18

commit v2 on v1

--- a/solution.py
+++ b/solution.py
@@ -10,7 +10,7 @@
 
 PAGE = 128
 SLOTS = 16
-UNROLL = 2
+UNROLL = 4
 MESH = pl.DeviceIdType.MESH
 
 
@@ -21,12 +21,12 @@
 def attend_kernel(
     length_ref, table_ref, migration_ref, dest_ref, query_ref, key_ref, value_ref,
     out_ref, key_area, value_area,
-    key_buf, value_buf, move_buf, zero_buf, page_sem, move_sem,
+    key_buf, value_buf, move_buf, zero_buf, query_buf, out_buf, page_sem, move_sem,
 ):
-    rows, max_pages = table_ref.shape
-    moves = migration_ref.shape[0]
+    max_pages, _, rows = table_ref.shape
+    moves = migration_ref.shape[1]
     kv_heads, _, page, head_dim = key_ref.shape
-    heads = query_ref.shape[1]
+    heads = query_ref.shape[1] // head_dim
     group = heads // kv_heads
     tokens = max_pages * page
     scale = 1.0 / math.sqrt(head_dim)
@@ -34,7 +34,7 @@
 
     def page_copies(row, index):
         slot = lax.rem(row, SLOTS)
-        source = table_ref[row, index]
+        source = table_ref[index, 0, row]
         place = pl.ds(index * page, page)
         return (
             pltpu.make_async_copy(
@@ -55,11 +55,11 @@
     def each_move(act):
         @pl.loop(0, moves)
         def _(move):
-            row, source = migration_ref[move, 0], migration_ref[move, 1]
+            row, source = migration_ref[0, move], migration_ref[1, move]
             for index in range(max_pages):
                 live = (source == me) & (index * page < length_ref[source, row])
-                slot = dest_ref[move, index]
-                act(move, index, live, table_ref[row, index], slot)
+                slot = dest_ref[index, move]
+                act(move, index, live, table_ref[index, 0, row], slot)
 
     def load_move(move, index, pool_page):
         return [
@@ -106,43 +106,35 @@
 
     each_move(begin_move)
 
+    query_buf[...] = jnp.zeros_like(query_buf)
+    for head in range(heads):
+        own = head // group * head_dim
+        query_buf[:, head, own : own + head_dim] = query_ref[
+            :, head * head_dim : (head + 1) * head_dim
+        ].astype(jnp.float32)
+
     position = lax.broadcasted_iota(jnp.int32, (heads, tokens), 1)
 
     def attend_row(row):
         slot = lax.rem(row, SLOTS)
-        keys = key_buf[slot].reshape(kv_heads * tokens, head_dim)
-        values = value_buf[slot].reshape(kv_heads * tokens, head_dim)
-        full = lax.dot_general(
-            query_ref[row], keys, (((1,), (1,)), ((), ())), preferred_element_type=jnp.float32
-        )
-        scores = jnp.concatenate(
+        keys = jnp.concatenate([key_buf[slot, k] for k in range(kv_heads)], axis=1)
+        values = jnp.concatenate([value_buf[slot, k] for k in range(kv_heads)], axis=1)
+        scores = lax.dot_general(
+            query_buf[row].astype(jnp.bfloat16), keys, (((1,), (1,)), ((), ())),
+            preferred_element_type=jnp.float32,
+        )
+        scores = jnp.where(position < length_ref[me, row], scores * scale, -1e30)
+        weights = jnp.exp(scores - jnp.max(scores, axis=-1, keepdims=True))
+        total = jnp.sum(weights, axis=-1, keepdims=True)
+        full = jnp.dot(weights.astype(jnp.bfloat16), values, preferred_element_type=jnp.float32)
+        mixed = jnp.concatenate(
             [
-                full[k * group : (k + 1) * group, k * tokens : (k + 1) * tokens]
+                full[k * group : (k + 1) * group, k * head_dim : (k + 1) * head_dim]
                 for k in range(kv_heads)
             ],
             axis=0,
         )
-        scores = jnp.where(position < length_ref[me, row], scores * scale, -1e30)
-        weights = jnp.exp(scores - jnp.max(scores, axis=-1, keepdims=True))
-        total = jnp.sum(weights, axis=-1, keepdims=True)
-        nothing = jnp.zeros((group, tokens), jnp.float32)
-        spread = jnp.concatenate(
-            [
-                jnp.concatenate(
-                    [
-                        weights[k * group : (k + 1) * group] if at == k else nothing
-                        for at in range(kv_heads)
-                    ],
-                    axis=1,
-                )
-                for k in range(kv_heads)
-            ],
-            axis=0,
-        )
-        mixed = jnp.dot(
-            spread.astype(jnp.bfloat16), values, preferred_element_type=jnp.float32
-        )
-        return (mixed / total).astype(out_ref.dtype)
+        return mixed / total
 
     steps = rows // UNROLL
 
@@ -152,7 +144,7 @@
             each_page(step * UNROLL + u, lambda copy: copy.wait())
         results = [attend_row(step * UNROLL + u) for u in range(UNROLL)]
         for u in range(UNROLL):
-            out_ref[step * UNROLL + u] = results[u]
+            out_buf[step * UNROLL + u] = results[u]
         for u in range(UNROLL):
             @pl.when(step * UNROLL + u + SLOTS < rows)
             def _():
@@ -174,14 +166,19 @@
         for copy in clear_move(move, index, slot):
             copy.wait()
 
+    for head in range(heads):
+        out_ref[:, head * head_dim : (head + 1) * head_dim] = out_buf[:, head].astype(
+            out_ref.dtype
+        )
+
     each_move(end_move)
 
 
 def attend(lengths, page_table, migration, dest_slots, queries, key_pages, value_pages):
-    rows, max_pages = page_table.shape
-    moves = migration.shape[0]
+    max_pages, _, rows = page_table.shape
+    moves = migration.shape[1]
     kv_heads, _, page, head_dim = key_pages.shape
-    heads = queries.shape[1]
+    heads = queries.shape[1] // head_dim
     area = jax.ShapeDtypeStruct((kv_heads, moves * max_pages, page, head_dim), key_pages.dtype)
     smem = pl.BlockSpec(memory_space=pltpu.SMEM)
     vmem = pl.BlockSpec(memory_space=pltpu.VMEM)
@@ -196,6 +193,8 @@
             pltpu.VMEM((SLOTS, kv_heads, max_pages * page, head_dim), key_pages.dtype),
             pltpu.VMEM((moves, max_pages, 2, kv_heads, page, head_dim), key_pages.dtype),
             pltpu.VMEM((kv_heads, page, head_dim), key_pages.dtype),
+            pltpu.VMEM((rows, heads, kv_heads * head_dim), jnp.float32),
+            pltpu.VMEM((rows, heads, head_dim), jnp.float32),
             pltpu.SemaphoreType.DMA((SLOTS, max_pages, 2)),
             pltpu.SemaphoreType.DMA((moves, max_pages, 2)),
         ],
@@ -344,17 +343,15 @@
 def body(lengths, page_table, migration, dest_slots, queries, key_cache, value_cache, out_weight):
     kv_heads = key_cache.shape[2]
     head_dim = key_cache.shape[4]
-    row_count = page_table.shape[1]
     pool_pages = key_cache.shape[3] // PAGE
-    heads = queries.shape[3] // head_dim
     key_pages = key_cache[0, 0].reshape(kv_heads, pool_pages, PAGE, head_dim)
     value_pages = value_cache[0, 0].reshape(kv_heads, pool_pages, PAGE, head_dim)
-    query_block = queries[0, 0].reshape(row_count, heads, head_dim)
     attended, key_area, value_area = attend(
-        lengths, page_table[0], migration, dest_slots, query_block, key_pages, value_pages
+        lengths, page_table.transpose(2, 0, 1), migration.T, dest_slots.T, queries[0, 0],
+        key_pages, value_pages,
     )
     got_keys, got_values = from_partner((key_area, value_area), "inst", 0)
-    update = project(attended.reshape(row_count, heads * head_dim), out_weight[0])
+    update = project(attended, out_weight[0])
     shape = (1, 1, kv_heads, got_keys.shape[1] * PAGE, head_dim)
     return (update[None], got_keys.reshape(shape), got_values.reshape(shape))
 

time: 62 us -> 55.1 us (0.89)
  local copies, waits for them, and re-layouts: 10.7 us -> 4.91 us
    unnamed x8 -> x5, local copies, waits for them, and re-layouts: 10.7 us -> 4.91 us
    pallas_call x1, Pallas kernels: 27.5 us -> 26.4 us  [attend(): pl.pallas_call(attend_kernel, out_shape=(jax.ShapeDtypeStruct(queries.sha...]
  transfers between devices with their start and end apart: 2 -> 2, of which waited for: 0 -> 0; matrix products, arithmetic and copies ran while one was open for 2% -> 0% of each run, Pallas kernels for 35% -> 40%
where the time goes in v2:
time: 55.1 us; the launch traced here: 55.2 us
  Pallas kernels  48.6 us (88%)
  local copies, waits for them, and re-layouts  4.91 us (9%)
  starting transfers between devices  1.05 us (2%)
  between operations  0.67 us (1%)
    pallas_call x1, Pallas kernels, attend(): pl.pallas_call(attend_kernel, out_shape=(jax.ShapeDtypeStruct(queries.sha...  26.4 us
    pallas_call x1, Pallas kernels, project(): pl.pallas_call(functools.partial(project_kernel, pipes, tensors), out_sha...  22.2 us
    unnamed x5, local copies, waits for them, and re-layouts  4.91 us
  transfers between devices with their start and end apart: 2, of which 0 were waited for; matrix products, arithmetic and copies ran while one was open for 0% of the time, Pallas kernels for 40%

profile of v2, /device:TPU:0, one launch (start us, length us, event | category | flops | bytes accessed | tf_op | source)
XLA Modules:
  0.0 55.2 jit_solution(9763517769085035755)
XLA Ops:
  0.6 26.4 %attend.1 = (bf16[64,2048]{1,0:T(8,128)(2,1)}, bf16[2,48,128,128]{3,2,1,0:T(8,128)(2,1)}, bf16[2,48,128,128]{3,2,1,0:T(8,128)(2,1)}) custom-call(s32[2,64]{1,0:T(2,128)} %length_ref.1, s32[3,1,64]{2,1,0:T(1,128)} %bitcast.19, s32[3,16]{1,0:T(4,128)} %bitcast.17, s32[3,16]{1,0:T(4,128)} %bitcast.18, bf16[64,2048]{1,0:T(8,128)(2,1)} %bitcast.16, ...), custom_call_target="tpu_custom_call" | custom-call | tf_op jit(solution)/shard_map/attend/pallas_call | solution.py:186
  27.1 1.0 %collective-permute-start = (bf16[2,48,128,128]{3,2,1,0:T(8,128)(2,1)}, bf16[2,48,128,128]{3,2,1,0:T(8,128)(2,1)S(1)}, u32[]{:S(2)}, u32[]{:S(2)}) collective-permute-start(bf16[2,48,128,128]{3,2,1,0:T(8,128)(2,1)} %get-tuple-element.7), channel_id=1, source_target_pairs={{0,16},{16,0},{1,17},{17,1},{2,18},{18,2},{3,19},{19,3},{4,20},{20... | collective-permute-start | bytes 9437192 | tf_op jit(solution)/shard_map/ppermute | solution.py:18
  28.0 0.1 collective-permute-start.1
  28.1 0.0 copy-start
  28.1 0.9 %copy-done = bf16[64,2048]{1,0:T(8,128)(2,1)S(1)} copy-done((bf16[64,2048]{1,0:T(8,128)(2,1)S(1)}, bf16[64,2048]{1,0:T(8,128)(2,1)}, u32[]{:S(2)}) %copy-start) | copy-done | bytes 262168
  29.1 22.2 %project.1 = bf16[64,512]{1,0:T(8,128)(2,1)S(1)} custom-call(bf16[64,2048]{1,0:T(8,128)(2,1)S(1)} %copy-done, bf16[2048,8192]{1,0:T(8,128)(2,1)} %bitcast.11), custom_call_target="tpu_custom_call" | custom-call | flops 2147483648 | bytes 33554432 | tf_op jit(solution)/shard_map/project/pallas_call | solution.py:313
  51.2 0.0 collective-permute-done
  51.2 0.0 collective-permute-done.1
  51.3 0.6 %copy.14 = bf16[1,64,512]{2,1,0:T(8,128)(2,1)} copy(bf16[1,64,512]{2,1,0:T(8,128)(2,1)S(1)} %bitcast.10) | data formatting | bytes 131072
  51.9 1.7 %copy.15 = bf16[1,1,2,6144,128]{4,3,2,1,0:T(8,128)(2,1)} copy(bf16[1,1,2,6144,128]{4,3,2,1,0:T(8,128)(2,1)S(1)} %bitcast.14) | data formatting | bytes 6291456
  53.6 1.7 %copy.16 = bf16[1,1,2,6144,128]{4,3,2,1,0:T(8,128)(2,1)} copy(bf16[1,1,2,6144,128]{4,3,2,1,0:T(8,128)(2,1)S(1)} %bitcast.15) | data formatting | bytes 6291456
Async XLA Ops:
  27.1 24.2 %collective-permute-start = (bf16[2,48,128,128]{3,2,1,0:T(8,128)(2,1)}, bf16[2,48,128,128]{3,2,1,0:T(8,128)(2,1)S(1)}, u32[]{:S(2)}, u32[]{:S(2)}) collective-permute-start(bf16[2,48,128,128]{3,2,1,0:T(8,128)(2,1)} %get-tuple-element.7), channel_id=1, source_target_pairs={{0,16},{16,0},{1,17},{17,1},{2,18},{18,2},{3,19},{19,3},{4,20},{20... | collective-permute-start | bytes 9437192 | tf_op jit(solution)/shard_map/ppermute | solution.py:18
  28.0 23.2 %collective-permute-start.1 = (bf16[2,48,128,128]{3,2,1,0:T(8,128)(2,1)}, bf16[2,48,128,128]{3,2,1,0:T(8,128)(2,1)S(1)}, u32[]{:S(2)}, u32[]{:S(2)}) collective-permute-start(bf16[2,48,128,128]{3,2,1,0:T(8,128)(2,1)} %get-tuple-element.8), channel_id=1, source_target_pairs={{0,16},{16,0},{1,17},{17,1},{2,18},{18,2},{3,19},{19,3},{4,20},{20... | collective-permute-start | bytes 9437192 | tf_op jit(solution)/shard_map/ppermute | solution.py:18
  28.1 0.9 %copy-start = (bf16[64,2048]{1,0:T(8,128)(2,1)S(1)}, bf16[64,2048]{1,0:T(8,128)(2,1)}, u32[]{:S(2)}) copy-start(bf16[64,2048]{1,0:T(8,128)(2,1)} %get-tuple-element.6.attended_ref) | copy-start | bytes 786436

commit v3 on v2

--- a/solution.py
+++ b/solution.py
@@ -185,7 +185,7 @@
     hbm = pl.BlockSpec(memory_space=pl.ANY)
     return pl.pallas_call(
         attend_kernel,
-        out_shape=(jax.ShapeDtypeStruct(queries.shape, queries.dtype), area, area),
+        out_shape=(pltpu.VMEM(queries.shape, queries.dtype), area, area),
         in_specs=[smem] * 4 + [vmem, hbm, hbm],
         out_specs=(vmem, hbm, hbm),
         scratch_shapes=[
@@ -340,6 +340,30 @@
     )(attended, weight)
 
 
+def land_kernel(keys_ref, values_ref, key_out, value_out, sem):
+    copies = [
+        pltpu.make_async_copy(keys_ref, key_out, sem.at[0]),
+        pltpu.make_async_copy(values_ref, value_out, sem.at[1]),
+    ]
+    for copy in copies:
+        copy.start()
+    for copy in copies:
+        copy.wait()
+
+
+def land(keys, values):
+    shape = jax.ShapeDtypeStruct(keys.shape, keys.dtype)
+    return pl.pallas_call(
+        land_kernel,
+        out_shape=(shape, shape),
+        in_specs=[pl.BlockSpec(memory_space=pltpu.VMEM)] * 2,
+        out_specs=[pl.BlockSpec(memory_space=pl.ANY)] * 2,
+        scratch_shapes=[pltpu.SemaphoreType.DMA((2,))],
+        compiler_params=pltpu.CompilerParams(vmem_limit_bytes=16 * 1024 * 1024),
+        name="land",
+    )(keys, values)
+
+
 def body(lengths, page_table, migration, dest_slots, queries, key_cache, value_cache, out_weight):
     kv_heads = key_cache.shape[2]
     head_dim = key_cache.shape[4]
@@ -352,6 +376,7 @@
     )
     got_keys, got_values = from_partner((key_area, value_area), "inst", 0)
     update = project(attended, out_weight[0])
+    got_keys, got_values = land(got_keys, got_values)
     shape = (1, 1, kv_heads, got_keys.shape[1] * PAGE, head_dim)
     return (update[None], got_keys.reshape(shape), got_values.reshape(shape))
 

time: 55.1 us -> 52.8 us (0.958)
  local copies, waits for them, and re-layouts: 4.91 us -> 0.63 us
  Pallas kernels: 48.6 us -> 50.6 us
    unnamed x5 -> x1, local copies, waits for them, and re-layouts: 4.91 us -> 0.63 us
    pallas_call x1 -> x2, Pallas kernels: 26.4 us -> 28.5 us  [the longest x1 25.7 us: attend(): pl.pallas_call(attend_kernel, out_shape=(pltpu.VMEM(queries.shape, querie...]
  transfers between devices with their start and end apart: 2 -> 2, of which waited for: 0 -> 0; matrix products, arithmetic and copies ran while one was open for 0% -> 0% of each run, Pallas kernels for 40% -> 42%
where the time goes in v3:
time: 52.8 us
  Pallas kernels  50.6 us (96%)
  starting transfers between devices  0.99 us (2%)
  between operations  0.67 us (1%)
  local copies, waits for them, and re-layouts  0.63 us (1%)
    pallas_call x1, Pallas kernels, attend(): pl.pallas_call(attend_kernel, out_shape=(pltpu.VMEM(queries.shape, querie...  25.7 us
    pallas_call x1, Pallas kernels, project(): pl.pallas_call(functools.partial(project_kernel, pipes, tensors), out_sha...  22.1 us
    pallas_call x1, Pallas kernels, land(): pl.pallas_call(land_kernel, out_shape=(shape, shape), in_specs=[pl.BlockS...  2.72 us
  transfers between devices with their start and end apart: 2, of which 0 were waited for; matrix products, arithmetic and copies ran while one was open for 0% of the time, Pallas kernels for 42%

profile of v3, /device:TPU:0, one launch (start us, length us, event | category | flops | bytes accessed | tf_op | source)
XLA Modules:
  0.0 52.8 jit_solution(6325988163437913047)
XLA Ops:
  0.6 25.7 %attend.1 = (bf16[64,2048]{1,0:T(8,128)(2,1)S(1)}, bf16[2,48,128,128]{3,2,1,0:T(8,128)(2,1)}, bf16[2,48,128,128]{3,2,1,0:T(8,128)(2,1)}) custom-call(s32[2,64]{1,0:T(2,128)} %length_ref.1, s32[3,1,64]{2,1,0:T(1,128)} %bitcast.17, s32[3,16]{1,0:T(4,128)} %bitcast.15, s32[3,16]{1,0:T(4,128)} %bitcast.16, bf16[64,2048]{1,0:T(8,128)(2,1)} %bitcast.14, ...), custom_call_target="tpu_custom_call" | custom-call | tf_op jit(solution)/shard_map/attend/pallas_call | solution.py:186
  26.4 0.9 %collective-permute-start = (bf16[2,48,128,128]{3,2,1,0:T(8,128)(2,1)}, bf16[2,48,128,128]{3,2,1,0:T(8,128)(2,1)S(1)}, u32[]{:S(2)}, u32[]{:S(2)}) collective-permute-start(bf16[2,48,128,128]{3,2,1,0:T(8,128)(2,1)} %get-tuple-element.9), channel_id=1, source_target_pairs={{0,16},{16,0},{1,17},{17,1},{2,18},{18,2},{3,19},{19,3},{4,20},{20... | collective-permute-start | bytes 9437192 | tf_op jit(solution)/shard_map/ppermute | solution.py:18
  27.3 0.1 collective-permute-start.1
  27.4 22.1 %project.1 = bf16[64,512]{1,0:T(8,128)(2,1)S(1)} custom-call(bf16[64,2048]{1,0:T(8,128)(2,1)S(1)} %get-tuple-element.8.attended_ref, bf16[2048,8192]{1,0:T(8,128)(2,1)} %bitcast.11), custom_call_target="tpu_custom_call" | custom-call | flops 2147483648 | bytes 33554432 | tf_op jit(solution)/shard_map/project/pallas_call | solution.py:313
  49.5 0.0 collective-permute-done.keys_ref
  49.5 0.0 collective-permute-done.1.values_ref
  49.5 2.7 %land.1 = (bf16[2,48,128,128]{3,2,1,0:T(8,128)(2,1)}, bf16[2,48,128,128]{3,2,1,0:T(8,128)(2,1)}) custom-call(bf16[2,48,128,128]{3,2,1,0:T(8,128)(2,1)S(1)} %collective-permute-done.keys_ref, bf16[2,48,128,128]{3,2,1,0:T(8,128)(2,1)S(1)} %collective-permute-done.1.values_ref), custom_call_target="tpu_custom_call" | custom-call | tf_op jit(solution)/shard_map/land/pallas_call | solution.py:356
  52.2 0.6 %copy.12 = bf16[1,64,512]{2,1,0:T(8,128)(2,1)} copy(bf16[1,64,512]{2,1,0:T(8,128)(2,1)S(1)} %bitcast.10) | data formatting | bytes 131072
Async XLA Ops:
  26.4 23.1 %collective-permute-start = (bf16[2,48,128,128]{3,2,1,0:T(8,128)(2,1)}, bf16[2,48,128,128]{3,2,1,0:T(8,128)(2,1)S(1)}, u32[]{:S(2)}, u32[]{:S(2)}) collective-permute-start(bf16[2,48,128,128]{3,2,1,0:T(8,128)(2,1)} %get-tuple-element.9), channel_id=1, source_target_pairs={{0,16},{16,0},{1,17},{17,1},{2,18},{18,2},{3,19},{19,3},{4,20},{20... | collective-permute-start | bytes 9437192 | tf_op jit(solution)/shard_map/ppermute | solution.py:18
  27.3 22.2 %collective-permute-start.1 = (bf16[2,48,128,128]{3,2,1,0:T(8,128)(2,1)}, bf16[2,48,128,128]{3,2,1,0:T(8,128)(2,1)S(1)}, u32[]{:S(2)}, u32[]{:S(2)}) collective-permute-start(bf16[2,48,128,128]{3,2,1,0:T(8,128)(2,1)} %get-tuple-element.10), channel_id=1, source_target_pairs={{0,16},{16,0},{1,17},{17,1},{2,18},{18,2},{3,19},{19,3},{4,20},{20... | collective-permute-start | bytes 9437192 | tf_op jit(solution)/shard_map/ppermute | solution.py:18
